TPU v7x, 32 devices: a whole 2x2x4 slice. The times are simulated.
32 devices in a mesh: groups: 2 (over y), space: 8 (over z, x), section: 2 (over core).
Axes of the slice: x: 2, y: 2, z: 4, core: 2. Of those that a mesh axis runs over, the one named last changes fastest.
Arguments:
- atm_state: bfloat16 [4, 8, 256, 256], P(('groups', 'section'), 'space'), parts along dimension 0, may hold values from -6 to 6
- ocean_state: bfloat16 [4, 2048, 192], P(('groups', 'section'), 'space'), parts along dimension 0, may hold values from -6 to 6
- owners: int32 [8, 256, 2], P('space'), may hold values from 0 to 7, all different within a row; in each aligned block of 256 rows (0 to 255, 256 to 511, ..., all dimensions but the last counted through in order) at most 128 rows name the same one
- target_cell: int32 [8, 256, 2], P('space'), may hold values from 0 to 255
- margin_weight: float32 [8, 256, 2], P('space'), may hold values from 0.25 to 1
- sea_mask: int32 [8, 256], P('space'), may hold values 0 or 1
- conv_kernel: bfloat16 [9, 256, 256], replicated, may hold values from -0.125 to 0.125
- meridional_weight: bfloat16 [256, 256], replicated, may hold values from -0.375 to 0.375
- atm_gain: float32 [256], replicated, may hold values from 0.25 to 1.75
- atm_in: bfloat16 [256, 1024], replicated, may hold values from -0.375 to 0.375
- atm_out: bfloat16 [1024, 256], replicated, may hold values from -0.1875 to 0.1875
- flux_weight: bfloat16 [256, 128], replicated, may hold values from -0.375 to 0.375
- forcing_weight: bfloat16 [128, 192], replicated, may hold values from -0.5 to 0.5
- ocean_gain: float32 [192], replicated, may hold values from 0.25 to 1.75
- ocean_in: bfloat16 [192, 768], replicated, may hold values from -0.4375 to 0.4375
- ocean_out: bfloat16 [768, 192], replicated, may hold values from -0.21875 to 0.21875
- surface_weight: bfloat16 [192, 128], replicated, may hold values from -0.4375 to 0.4375
- feedback_weight: bfloat16 [128, 256], replicated, may hold values from -0.5 to 0.5
Outputs:
- atm_next: bfloat16 [4, 8, 256, 256], P(('groups', 'section'), 'space'), parts along dimension 0
- ocean_next: bfloat16 [4, 2048, 192], P(('groups', 'section'), 'space'), parts along dimension 0
There are 2 independent parts, one for each index of `groups`. A program takes and returns all parts, laid end to end along the dimension named above; an argument that names none is the same for every part. Nothing has to cross between parts.
Inputs may be any that keep to these rules, and one draw needn't show every extreme that they name: Within the 256 cells of one latitude band, no owner is named by more than 128 margin entries, a bound that some block reaches; the 2 owners of one cell differ.
All inputs are finite; a program needn't handle non-finite values. No bound on the sum of `sea_mask` on one device may be relied on, other than what follows from the above.
Results may differ from a plain program's by a relative error of at most 0.014.
Values may be sent and summed in bfloat16 or wider, within the bound.
A program may use at most 64 MiB of HBM per device.

v0:
```python
import math
import jax
import jax.numpy as jnp
from jax import lax
from jax.sharding import PartitionSpec as P


def extended(cells, sides, width):
    for axis, dim in sides:
        count = lax.axis_size(axis)
        ends = count - 1
        head = lax.slice_in_dim(cells, 0, width, axis=dim)
        tail = lax.slice_in_dim(cells, cells.shape[dim] - width, cells.shape[dim], axis=dim)
        cells = jnp.concatenate(
            [
                lax.ppermute(tail, axis, [(i, (i + 1) % count) for i in range(ends)]),
                cells,
                lax.ppermute(head, axis, [((i + 1) % count, i) for i in range(ends)]),
            ],
            axis=dim,
        )
    return cells


def entering(part, axis, combine, identity):
    place = lax.axis_index(axis)
    gathered = lax.all_gather(part, axis)
    state = jnp.zeros_like(part) + jnp.asarray(identity, part.dtype)

    def one(hop, state):
        return combine(state, lax.dynamic_index_in_dim(gathered, hop, 0, False))

    return lax.fori_loop(0, place, one, state)


def conv_taps(padded, kernel, lat_rows):
    channels = padded.shape[-1]
    columns = []
    for row_off in range(3):
        lat_band = padded[row_off : row_off + lat_rows]
        for col_off in range(3):
            columns.append(jnp.roll(lat_band, 1 - col_off, axis=1))
    stacked = jnp.concatenate(columns, axis=-1)
    flattened = stacked.reshape(-1, 9 * channels)
    result = jnp.dot(
        flattened, kernel.reshape(9 * channels, channels), preferred_element_type=jnp.float32
    )
    return result.reshape(lat_rows, padded.shape[1], channels)


def rms_scale(values, gain_vec):
    return values * lax.rsqrt(jnp.mean(values * values, axis=-1, keepdims=True) + 1e-06) * gain_vec


def add_terms(earlier, later):
    return earlier + later


def contract_first(left, right):
    return lax.dot_general(
        left, right, (((0,), (0,)), ((), ())), preferred_element_type=jnp.float32
    )


def local(
    atm_state,
    ocean_state,
    owners,
    target_cell,
    margin_weight,
    sea_mask,
    conv_kernel,
    meridional_weight,
    atm_gain,
    atm_in,
    atm_out,
    flux_weight,
    forcing_weight,
    ocean_gain,
    ocean_in,
    ocean_out,
    surface_weight,
    feedback_weight,
):
    atm_one = atm_state[0]
    ocn_one = ocean_state[0]
    lat_rows, lon_cells, channels = atm_one.shape
    margin_count = owners.shape[-1]
    flux_width = flux_weight.shape[1]
    peer_count = lax.axis_size("space")
    slot_count = max(2, 2 * lat_rows * lon_cells * margin_count // peer_count)
    lat_total = lat_rows * peer_count
    padded = extended(atm_one, (("space", 0),), 1)
    mixing = conv_taps(padded, conv_kernel, lat_rows)
    hidden = atm_one.astype(jnp.float32) + mixing
    zonal_sums = jnp.sum(hidden, axis=1) / math.sqrt(lon_cells)
    band_total = jnp.sum(zonal_sums, axis=0)
    before = entering(band_total, "space", add_terms, jnp.zeros_like(band_total))
    prefix = (before[None, :] + jnp.cumsum(zonal_sums, axis=0) - zonal_sums) / math.sqrt(lat_total)
    meridional = jnp.dot(
        prefix, meridional_weight.astype(jnp.float32), precision=lax.Precision.HIGHEST
    )
    lifted = (hidden + meridional[:, None, :]).reshape(-1, channels)
    normed = rms_scale(lifted, atm_gain).astype(jnp.bfloat16)
    activated = jax.nn.silu(jnp.dot(normed, atm_in, preferred_element_type=jnp.float32)).astype(
        jnp.bfloat16
    )
    atm_mid = (lifted + jnp.dot(activated, atm_out, preferred_element_type=jnp.float32)).astype(
        jnp.bfloat16
    )
    flux_rows = jnp.dot(atm_mid, flux_weight, preferred_element_type=jnp.float32)
    sea_cells = sea_mask.astype(jnp.float32).reshape(-1)
    weights = margin_weight.reshape(-1, margin_count)
    payload = (weights[:, :, None] * sea_cells[:, None, None] * flux_rows[:, None, :]).astype(
        jnp.bfloat16
    )
    payload = payload.reshape(-1, flux_width)
    owner_ids = owners.reshape(-1)
    owner_hits = (owner_ids[:, None] == jnp.arange(peer_count, dtype=jnp.int32)[None, :]).astype(
        jnp.int32
    )
    slot_rank = jnp.sum((jnp.cumsum(owner_hits, axis=0) - 1) * owner_hits, axis=1)
    slot_index = owner_ids * slot_count + slot_rank
    slot_total = peer_count * slot_count
    placement = slot_index[:, None] == jnp.arange(slot_total, dtype=jnp.int32)[None, :]
    place_bf = placement.astype(jnp.bfloat16)
    send_rows = contract_first(place_bf, payload).astype(jnp.bfloat16)
    entry_cells = target_cell.reshape(-1)
    send_cells = jnp.sum(placement.astype(jnp.int32) * entry_cells[:, None], axis=0)
    recv_rows, recv_cells = (
        lax.all_to_all(
            send_rows.reshape(peer_count, slot_count, flux_width),
            "space",
            split_axis=0,
            concat_axis=0,
            tiled=True,
        ),
        lax.all_to_all(
            send_cells.reshape(peer_count, slot_count),
            "space",
            split_axis=0,
            concat_axis=0,
            tiled=True,
        ),
    )
    recv_cells = recv_cells.reshape(-1)
    ocean_cells = ocn_one.shape[0]
    cell_onehot = (recv_cells[:, None] == jnp.arange(ocean_cells, dtype=jnp.int32)[None, :]).astype(
        jnp.bfloat16
    )
    forcing = contract_first(cell_onehot, recv_rows.reshape(-1, flux_width)).astype(jnp.bfloat16)
    ocean_lift = ocn_one.astype(jnp.float32) + jnp.dot(
        forcing, forcing_weight, preferred_element_type=jnp.float32
    )
    ocean_normed = rms_scale(ocean_lift, ocean_gain).astype(jnp.bfloat16)
    ocean_act = jax.nn.silu(
        jnp.dot(ocean_normed, ocean_in, preferred_element_type=jnp.float32)
    ).astype(jnp.bfloat16)
    ocean_new = (
        ocean_lift + jnp.dot(ocean_act, ocean_out, preferred_element_type=jnp.float32)
    ).astype(jnp.bfloat16)
    surface = jnp.dot(ocean_new, surface_weight, preferred_element_type=jnp.float32).astype(
        jnp.bfloat16
    )
    back_rows = jnp.dot(cell_onehot, surface, preferred_element_type=jnp.float32).astype(
        jnp.bfloat16
    )
    returned = lax.all_to_all(
        back_rows.reshape(peer_count, slot_count, flux_width),
        "space",
        split_axis=0,
        concat_axis=0,
        tiled=True,
    )
    picked = jnp.dot(place_bf, returned.reshape(-1, flux_width), preferred_element_type=jnp.float32)
    picked = picked.reshape(-1, margin_count, flux_width)
    feedback = jnp.sum(weights[:, :, None] * picked, axis=1).astype(jnp.bfloat16)
    back_term = jnp.dot(feedback, feedback_weight, preferred_element_type=jnp.float32)
    atm_new = (atm_mid.astype(jnp.float32) + sea_cells[:, None] * back_term).astype(jnp.bfloat16)
    return (atm_new.reshape(1, lat_rows, lon_cells, channels), ocean_new[None])


def solution(mesh):
    placed = (
        P(("groups", "section"), "space", None, None),
        P(("groups", "section"), "space", None),
        P("space", None, None),
        P("space", None, None),
        P("space", None, None),
        P("space", None),
        P(),
        P(),
        P(),
        P(),
        P(),
        P(),
        P(),
        P(),
        P(),
        P(),
        P(),
        P(),
    )
    return jax.shard_map(
        local,
        mesh=mesh,
        in_specs=placed,
        out_specs=(
            P(("groups", "section"), "space", None, None),
            P(("groups", "section"), "space", None),
        ),
        check_vma=False,
    )
```

profile of v0, /device:TPU:0, one launch (start us, length us, event | category | flops | bytes accessed | tf_op | source)
XLA Modules:
  0.0 71.0 jit_solution(671286517310417763)
XLA Ops:
  0.6 0.0 copy-start
  0.6 0.0 copy-start.1
  0.7 5.0 %collective-permute-start = (bf16[1,256,256]{2,1,0:T(8,128)(2,1)}, bf16[1,256,256]{2,1,0:T(8,128)(2,1)S(1)}, u32[]{:S(2)}, u32[]{:S(2)}) collective-permute-start(bf16[1,256,256]{2,1,0:T(8,128)(2,1)} %bitcast.71), channel_id=1, source_target_pairs={{0,2},{2,4},{4,6},{6,8},{8,10},{10,12},{12,14},{1,3},{3,5},{5,7},{... | collective-permute-start | bytes 393224 | tf_op jit(solution)/shard_map/ppermute | solution.py:16
  5.7 1.3 %collective-permute-start.1 = (bf16[1,256,256]{2,1,0:T(8,128)(2,1)}, bf16[1,256,256]{2,1,0:T(8,128)(2,1)S(1)}, u32[]{:S(2)}, u32[]{:S(2)}) collective-permute-start(bf16[1,256,256]{2,1,0:T(8,128)(2,1)} %bitcast.72), channel_id=1, source_target_pairs={{2,0},{4,2},{6,4},{8,6},{10,8},{12,10},{14,12},{3,1},{5,3},{7,5},{... | collective-permute-start | bytes 393224 | tf_op jit(solution)/shard_map/ppermute | solution.py:18
  7.0 0.8 %copy.35 = s32[1,256,2]{2,1,0:T(8,128)S(1)} copy(s32[1,256,2]{1,2,0:T(2,128)} %param.22) | data formatting | bytes 4096 | tf_op args[2]
  7.8 0.1 eq.79
  8.0 0.1 eq.75
  8.1 1.1 %reduce-window.6 = s32[8,4,128]{2,0,1:T(8,128)S(1)} reduce-window(s32[8,4,128]{2,0,1:T(8,128)S(1)} %fusion.41, s32[]{:T(128)} %constant.39.clone.1), window={size=1x1x128 pad=0_0x0_0x127_0}, to_apply=%region_4.5 | reduce-window | flops 520192 | bytes 32772 | tf_op jit(solution)/shard_map/reduce-window
  9.3 0.2 slice_reduce_fusion
  9.5 0.1 fusion.40
  9.6 0.8 %copy.39 = s32[1,256,2]{2,1,0:T(8,128)S(1)} copy(s32[1,256,2]{1,2,0:T(2,128)} %param.23) | data formatting | bytes 4096 | tf_op args[3]
  10.4 0.1 mul.144
  10.6 0.9 %select_reduce_fusion = s32[1024]{0:T(1024)} fusion(s32[512]{0:T(512)S(1)} %mul.144, s32[512]{0:T(512)S(1)} %multiply_add_fusion), kind=kLoop, calls=%fused_computation.1 | loop fusion | flops 1571840 | bytes 8192 | tf_op jit(solution)/shard_map/reduce_sum | solution.py:129
  11.5 7.0 %all-to-all-start = ((s32[8,1,128]{2,1,0:T(1,128)}), s32[8,1,128]{2,1,0:T(1,128)S(1)}, u32[]{:S(2)}, u32[]{:S(2)}) async-start(s32[8,1,128]{2,1,0:T(1,128)} %bitcast.14), calls=%async_computation | async-start | bytes 8192 | tf_op jit(solution)/shard_map/all_to_all | solution.py:138
  18.4 1.0 %fusion.47 = (bf16[1,255,256]{2,1,0:T(8,128)(2,1)S(1)}, bf16[1,255,256]{2,1,0:T(8,128)(2,1)S(1)}) fusion(bf16[1,256,256]{2,1,0:T(8,128)(2,1)} %bitcast.73), kind=kLoop, calls=%fused_computation.73 | loop fusion | bytes 522240 | tf_op jit(solution)/shard_map/jit(_roll_static)/slice | solution.py:42
  19.5 0.1 mul.147
  19.6 0.1 mul.148
  19.7 0.1 copy.40
  19.9 0.1 broadcast_in_dim_reshape.2
  20.4 0.0 copy-start.2
  20.5 0.0 copy-start.7
  20.5 0.0 copy-start.8
  20.5 0.0 copy-start.14
  20.5 0.5 fusion.51
  21.0 21.0 %all-gather.1 = f32[8,1,256]{2,1,0:T(1,128)S(1)} all-gather(f32[1,1,256]{2,1,0:T(1,128)S(1)} %bitcast.86), channel_id=2, replica_groups=mesh['groups'=2,'space'=8,'section'=2] {'space'}, dimensions={0}, use_global_device_ids=true | all-gather | bytes 9216 | tf_op jit(solution)/shard_map/all_gather | solution.py:27
  42.0 0.1 fusion.52
  42.2 0.2 multiply_reduce_fusion
  42.4 0.0 copy-start.3
  42.4 0.6 fusion.18
  43.0 0.2 copy-done.3
  43.2 0.2 fusion.53
  43.4 0.1 mul.151
  43.5 0.0 copy-start.9
  43.5 0.0 copy-start.10
  43.5 0.0 copy-start.15
  43.5 0.9 %fusion.4 = bf16[1024,128]{1,0:T(8,128)(2,1)S(1)} fusion(s32[512]{0:T(512)S(1)} %multiply_add_fusion, f32[512,128]{1,0:T(8,128)S(1)} %bitcast.75, f32[512]{0:T(512)S(1)} %mul.149), kind=kOutput, calls=%fused_computation.7 | convolution fusion | flops 135004160 | bytes 528384 | tf_op jit(solution)/shard_map/dot_general | solution.py:60
  44.4 10.6 %all_to_all.19 = bf16[8,128,128]{2,1,0:T(8,128)(2,1)S(1)} all-to-all(bf16[8,128,128]{2,1,0:T(8,128)(2,1)S(1)} %bitcast.77), channel_id=1, replica_groups=mesh['groups'=2,'space'=8,'section'=2] {'space'}, dimensions={0} | all-to-all | bytes 524288 | tf_op jit(solution)/shard_map/all_to_all | solution.py:131
  55.1 0.8 %multiply_reduce_fusion.1 = (f32[256]{0:T(256)S(1)}, f32[256,192]{0,1:T(8,128)S(1)}) fusion(bf16[128,192]{0,1:T(8,128)(2,1)S(1)} %copy-done.12, bf16[1024,128]{1,0:T(8,128)(2,1)S(1)} %bitcast.78, s32[1024]{0:T(1024)S(1)} %bitcast.87, bf16[1,256,192]{1,2,0:T(8,128)(2,1)S(1)} %copy-done.11), kind=kOutput, calls=%fused_computation.37 | convolution fusion | flops 80183040 | bytes 611328 | tf_op jit(solution)/shard_map/dot_general | solution.py:152
  55.9 0.0 copy-start.13
  55.9 0.7 fusion.19
  56.6 0.1 copy-done.13
  56.7 1.2 %convolution_convert_fusion = bf16[1024,128]{1,0:T(8,128)(2,1)} fusion(bf16[256,192]{0,1:T(8,128)(2,1)S(1)} %fusion.19, bf16[192,128]{1,0:T(8,128)(2,1)S(1)} %copy-done.13, s32[1024]{0:T(1024)S(1)} %bitcast.88), kind=kOutput, calls=%fused_computation.8 | convolution fusion | flops 80117760 | bytes 413696 | tf_op jit(solution)/shard_map/dot_general | solution.py:165
  58.0 3.5 %all-to-all-start.2 = ((bf16[8,128,128]{2,1,0:T(8,128)(2,1)}), bf16[8,128,128]{2,1,0:T(8,128)(2,1)S(1)}, u32[]{:S(2)}, u32[]{:S(2)}) async-start(bf16[8,128,128]{2,1,0:T(8,128)(2,1)} %bitcast.20), calls=%async_computation.2 | async-start | bytes 524288 | tf_op jit(solution)/shard_map/all_to_all | solution.py:168
  61.5 0.1 reduce_sum.63
  61.7 0.1 copy.38
  61.8 7.9 %all-to-all-done.2 = bf16[8,128,128]{2,1,0:T(8,128)(2,1)S(1)} async-done(((bf16[8,128,128]{2,1,0:T(8,128)(2,1)}), bf16[8,128,128]{2,1,0:T(8,128)(2,1)S(1)}, u32[]{:S(2)}, u32[]{:S(2)}) %all-to-all-start.2) | async-done | bytes 262176 | tf_op jit(solution)/shard_map/all_to_all | solution.py:168
  69.7 0.5 fusion.15
  70.2 0.8 %fusion.20 = bf16[1,1,256,256]{3,2,1,0:T(8,128)(2,1)} fusion(bf16[128,256]{1,0:T(8,128)(2,1)S(1)} %copy-done.4, bf16[256,256]{1,0:T(8,128)(2,1)S(1)} %fusion.18, f32[256]{0:T(256)S(1)} %bitcast.82, bf16[256,128]{1,0:T(8,128)(2,1)S(1)} %fusion.15), kind=kOutput, calls=%fused_computation.22 | convolution fusion | flops 17039360 | bytes 394240 | tf_op jit(solution)/shard_map/dot_general | solution.py:178
  (52 shorter events, 0.4 us)
Async XLA Ops:
  0.6 19.8 %copy-start = (bf16[9,256,256]{2,1,0:T(8,128)(2,1)S(1)}, bf16[9,256,256]{2,1,0:T(8,128)(2,1)}, u32[]{:S(2)}) copy-start(bf16[9,256,256]{2,1,0:T(8,128)(2,1)} %param.26) | copy-start | bytes 3538948
  0.6 19.4 %copy-start.1 = (bf16[1,1,256,256]{3,2,1,0:T(8,128)(2,1)S(1)}, bf16[1,1,256,256]{3,2,1,0:T(8,128)(2,1)}, u32[]{:S(2)}) copy-start(bf16[1,1,256,256]{3,2,1,0:T(8,128)(2,1)} %param.20) | copy-start | bytes 393220
  0.7 18.8 %copy-start.6 = (s32[1,256]{1,0:T(1,128)S(1)}, s32[1,256]{1,0:T(1,128)}, u32[]{:S(2)}) copy-start(s32[1,256]{1,0:T(1,128)} %param.25) | copy-start | bytes 3076
  0.7 19.1 %copy-start.5 = (f32[1,256,2]{1,2,0:T(2,128)S(1)}, f32[1,256,2]{1,2,0:T(2,128)}, u32[]{:S(2)}) copy-start(f32[1,256,2]{1,2,0:T(2,128)} %param.24) | copy-start | bytes 6148
  0.7 19.4 %collective-permute-start = (bf16[1,256,256]{2,1,0:T(8,128)(2,1)}, bf16[1,256,256]{2,1,0:T(8,128)(2,1)S(1)}, u32[]{:S(2)}, u32[]{:S(2)}) collective-permute-start(bf16[1,256,256]{2,1,0:T(8,128)(2,1)} %bitcast.71), channel_id=1, source_target_pairs={{0,2},{2,4},{4,6},{6,8},{8,10},{10,12},{12,14},{1,3},{3,5},{5,7},{... | collective-permute-start | bytes 393224 | tf_op jit(solution)/shard_map/ppermute | solution.py:16
  5.7 14.6 %collective-permute-start.1 = (bf16[1,256,256]{2,1,0:T(8,128)(2,1)}, bf16[1,256,256]{2,1,0:T(8,128)(2,1)S(1)}, u32[]{:S(2)}, u32[]{:S(2)}) collective-permute-start(bf16[1,256,256]{2,1,0:T(8,128)(2,1)} %bitcast.72), channel_id=1, source_target_pairs={{2,0},{4,2},{6,4},{8,6},{10,8},{12,10},{14,12},{3,1},{5,3},{7,5},{... | collective-permute-start | bytes 393224 | tf_op jit(solution)/shard_map/ppermute | solution.py:18
  11.5 32.9 %all-to-all-start = ((s32[8,1,128]{2,1,0:T(1,128)}), s32[8,1,128]{2,1,0:T(1,128)S(1)}, u32[]{:S(2)}, u32[]{:S(2)}) async-start(s32[8,1,128]{2,1,0:T(1,128)} %bitcast.14), calls=%async_computation | async-start | bytes 8192 | tf_op jit(solution)/shard_map/all_to_all | solution.py:138
  20.4 21.6 %copy-start.2 = (bf16[256,256]{1,0:T(8,128)(2,1)S(1)}, bf16[256,256]{1,0:T(8,128)(2,1)}, u32[]{:S(2)}) copy-start(bf16[256,256]{1,0:T(8,128)(2,1)} %param.27) | copy-start | bytes 393220
  20.5 21.9 %copy-start.7 = (bf16[1024,256]{1,0:T(8,128)(2,1)S(1)}, bf16[1024,256]{1,0:T(8,128)(2,1)}, u32[]{:S(2)}) copy-start(bf16[1024,256]{1,0:T(8,128)(2,1)} %param.30) | copy-start | bytes 1572868
  20.5 21.9 %copy-start.8 = (bf16[256,1024]{1,0:T(8,128)(2,1)S(1)}, bf16[256,1024]{1,0:T(8,128)(2,1)}, u32[]{:S(2)}) copy-start(bf16[256,1024]{1,0:T(8,128)(2,1)} %param.29) | copy-start | bytes 1572868
  20.5 21.9 %copy-start.14 = (f32[256]{0:T(256)S(1)}, f32[256]{0:T(256)}, u32[]{:S(2)}) copy-start(f32[256]{0:T(256)} %param.28) | copy-start | bytes 3076
  42.4 0.8 %copy-start.3 = (bf16[256,128]{1,0:T(8,128)(2,1)S(1)}, bf16[256,128]{1,0:T(8,128)(2,1)}, u32[]{:S(2)}) copy-start(bf16[256,128]{1,0:T(8,128)(2,1)} %param.31) | copy-start | bytes 196612
  43.2 11.9 %copy-start.11 = (bf16[1,256,192]{1,2,0:T(8,128)(2,1)S(1)}, bf16[1,256,192]{1,2,0:T(8,128)(2,1)}, u32[]{:S(2)}) copy-start(bf16[1,256,192]{1,2,0:T(8,128)(2,1)} %param.21) | copy-start | bytes 294916
  43.2 11.9 %copy-start.12 = (bf16[128,192]{0,1:T(8,128)(2,1)S(1)}, bf16[128,192]{0,1:T(8,128)(2,1)}, u32[]{:S(2)}) copy-start(bf16[128,192]{0,1:T(8,128)(2,1)} %param.32) | copy-start | bytes 147460
  43.5 12.4 %copy-start.9 = (bf16[768,192]{0,1:T(8,128)(2,1)S(1)}, bf16[768,192]{0,1:T(8,128)(2,1)}, u32[]{:S(2)}) copy-start(bf16[768,192]{0,1:T(8,128)(2,1)} %param.35) | copy-start | bytes 884740
  43.5 12.4 %copy-start.10 = (bf16[192,768]{1,0:T(8,128)(2,1)S(1)}, bf16[192,768]{1,0:T(8,128)(2,1)}, u32[]{:S(2)}) copy-start(bf16[192,768]{1,0:T(8,128)(2,1)} %param.34) | copy-start | bytes 884740
  43.5 12.4 %copy-start.15 = (f32[192]{0:T(256)S(1)}, f32[192]{0:T(256)}, u32[]{:S(2)}) copy-start(f32[192]{0:T(256)} %param.33) | copy-start | bytes 2308
  55.9 0.8 %copy-start.13 = (bf16[192,128]{1,0:T(8,128)(2,1)S(1)}, bf16[192,128]{1,0:T(8,128)(2,1)}, u32[]{:S(2)}) copy-start(bf16[192,128]{1,0:T(8,128)(2,1)} %param.36) | copy-start | bytes 147460
  56.7 13.5 %copy-start.16 = (bf16[256,192]{0,1:T(8,128)(2,1)}, bf16[256,192]{0,1:T(8,128)(2,1)S(1)}, u32[]{:S(2)}) copy-start(bf16[256,192]{0,1:T(8,128)(2,1)S(1)} %fusion.19) | copy-start | bytes 294916
  58.0 12.2 %copy-start.4 = (bf16[128,256]{1,0:T(8,128)(2,1)S(1)}, bf16[128,256]{1,0:T(8,128)(2,1)}, u32[]{:S(2)}) copy-start(bf16[128,256]{1,0:T(8,128)(2,1)} %param.37) | copy-start | bytes 196612
  58.0 11.7 %all-to-all-start.2 = ((bf16[8,128,128]{2,1,0:T(8,128)(2,1)}), bf16[8,128,128]{2,1,0:T(8,128)(2,1)S(1)}, u32[]{:S(2)}, u32[]{:S(2)}) async-start(bf16[8,128,128]{2,1,0:T(8,128)(2,1)} %bitcast.20), calls=%async_computation.2 | async-start | bytes 524288 | tf_op jit(solution)/shard_map/all_to_all | solution.py:168
where the time goes:
time: 71.6 us; the launch traced here: 71 us
  blocking collectives  31.6 us (44%)
  starting transfers between devices  16.8 us (23%)
  waiting for transfers between devices  7.92 us (11%)
  matrix products  6.33 us (9%)
  local copies, waits for them, and re-layouts  4.64 us (6%)
  other arithmetic  2.53 us (4%)
  between operations  1.17 us (2%)
    all_gather x1, blocking collectives, entering(): gathered = lax.all_gather(part, axis)  21 us
    all_to_all x1, blocking collectives, local(): lax.all_to_all(send_rows.reshape(peer_count, slot_count, flux_width), 'sp...  10.6 us
    all_to_all x1, waiting for transfers between devices, local(): lax.all_to_all(back_rows.reshape(peer_count, slot_count, flux_width), 'sp...  7.91 us
    all_to_all x1, starting transfers between devices, local(): lax.all_to_all(send_cells.reshape(peer_count, slot_count), 'space', split...  6.96 us
    ppermute x1, starting transfers between devices, extended(): lax.ppermute(tail, axis, [(i, (i + 1) % count) for i in range(ends)])  5.01 us
    all_to_all x1, starting transfers between devices, local(): lax.all_to_all(back_rows.reshape(peer_count, slot_count, flux_width), 'sp...  3.54 us
    unnamed x41, local copies, waits for them, and re-layouts  2.22 us
  transfers between devices with their start and end apart: 4, of which 1 were waited for; matrix products, arithmetic and copies ran while one was open for 13% of the time, Pallas kernels for 0%

commit v1 on v0

--- a/solution.py
+++ b/solution.py
@@ -3,6 +3,25 @@
 import jax.numpy as jnp
 from jax import lax
 from jax.sharding import PartitionSpec as P
+
+
+def connect_pools(q_in, axis_no, piece_in):
+    p_next = q_in.shape
+    return jnp.moveaxis(
+        q_in.reshape(
+            *p_next[:axis_no], piece_in, p_next[axis_no] // piece_in, *p_next[axis_no + 1 :]
+        ),
+        axis_no,
+        0,
+    )
+
+
+def connect_classes(sample, array_axis):
+    sample = jnp.moveaxis(sample, 0, array_axis)
+    then = sample.shape
+    return sample.reshape(
+        *then[:array_axis], then[array_axis] * then[array_axis + 1], *then[array_axis + 2 :]
+    )
 
 
 def extended(cells, sides, width):
@@ -127,6 +146,26 @@
     send_rows = contract_first(place_bf, payload).astype(jnp.bfloat16)
     entry_cells = target_cell.reshape(-1)
     send_cells = jnp.sum(placement.astype(jnp.int32) * entry_cells[:, None], axis=0)
+
+    def update_leaves(target, named_axis, v0, s0):
+        y = lax.axis_size(named_axis)
+        e_now, local_now = (y, lax.axis_index(named_axis))
+        shaped = connect_pools(target, v0, e_now)
+        row_list = [shaped[local_now]]
+        tick = 1
+        while tick < e_now:
+            b_now = shaped[(local_now + tick) % e_now]
+            row_list.append(
+                lax.ppermute(
+                    b_now,
+                    axis_name=named_axis,
+                    perm=[(nth, (nth + tick) % e_now) for nth in range(e_now)],
+                )
+            )
+            tick = tick + 1
+        shaped = jnp.stack(row_list, 0)[(local_now - jnp.arange(e_now)) % e_now]
+        return connect_classes(shaped, s0)
+
     recv_rows, recv_cells = (
         lax.all_to_all(
             send_rows.reshape(peer_count, slot_count, flux_width),
@@ -135,13 +174,7 @@
             concat_axis=0,
             tiled=True,
         ),
-        lax.all_to_all(
-            send_cells.reshape(peer_count, slot_count),
-            "space",
-            split_axis=0,
-            concat_axis=0,
-            tiled=True,
-        ),
+        update_leaves(send_cells.reshape(peer_count, slot_count), "space", 0, 0),
     )
     recv_cells = recv_cells.reshape(-1)
     ocean_cells = ocn_one.shape[0]

time: 71.6 us -> 76.8 us (1.073)
  starting transfers between devices: 16.8 us -> 27.9 us
  blocking collectives: 31.6 us -> 22 us
  waiting for transfers between devices: 7.92 us -> 10.1 us
    ppermute x0 -> x7, starting transfers between devices: none -> 12.6 us  [update_leaves(): lax.ppermute(b_now, axis_name=named_axis, perm=[(nth, (nth + tick) % e_no...]
    all_to_all x1 -> x0, blocking collectives: 10.6 us -> none  [local(): lax.all_to_all(send_rows.reshape(peer_count, slot_count, flux_width), 'sp...]
    all_to_all x1, starting transfers between devices: 6.96 us -> 3.41 us  [local(): lax.all_to_all(send_rows.reshape(peer_count, slot_count, flux_width), 'sp...]
    ppermute x0 -> x7, waiting for transfers between devices: none -> 2.09 us  [update_leaves(): lax.ppermute(b_now, axis_name=named_axis, perm=[(nth, (nth + tick) % e_no...]
    all_to_all x1, starting transfers between devices: 3.54 us -> 5.56 us  [local(): lax.all_to_all(back_rows.reshape(peer_count, slot_count, flux_width), 'sp...]
    all_gather x1, blocking collectives: 21 us -> 22 us  [entering(): gathered = lax.all_gather(part, axis)]
  transfers between devices with their start and end apart: 4 -> 11, of which waited for: 1 -> 3; matrix products, arithmetic and copies ran while one was open for 13% -> 9% of each run, Pallas kernels for 0% -> 0%
where the time goes in v1:
time: 76.8 us; the launch traced here: 76.2 us
  starting transfers between devices  27.9 us (36%)
  blocking collectives  22 us (29%)
  waiting for transfers between devices  10.1 us (13%)
  matrix products  7.04 us (9%)
  local copies, waits for them, and re-layouts  5.27 us (7%)
  other arithmetic  2.61 us (3%)
  between operations  1.32 us (2%)
    all_gather x1, blocking collectives, entering(): gathered = lax.all_gather(part, axis)  22 us
    ppermute x7, starting transfers between devices, update_leaves(): lax.ppermute(b_now, axis_name=named_axis, perm=[(nth, (nth + tick) % e_no...  12.6 us
    all_to_all x1, waiting for transfers between devices, local(): lax.all_to_all(back_rows.reshape(peer_count, slot_count, flux_width), 'sp...  7.98 us
    all_to_all x1, starting transfers between devices, local(): lax.all_to_all(back_rows.reshape(peer_count, slot_count, flux_width), 'sp...  5.56 us
    ppermute x1, starting transfers between devices, extended(): lax.ppermute(tail, axis, [(i, (i + 1) % count) for i in range(ends)])  5.01 us
    all_to_all x1, starting transfers between devices, local(): lax.all_to_all(send_rows.reshape(peer_count, slot_count, flux_width), 'sp...  3.41 us
    ppermute x7, waiting for transfers between devices, update_leaves(): lax.ppermute(b_now, axis_name=named_axis, perm=[(nth, (nth + tick) % e_no...  2.09 us
    slice x6, local copies, waits for them, and re-layouts, conv_taps(): columns.append(jnp.roll(lat_band, 1 - col_off, axis=1))  1.81 us
  transfers between devices with their start and end apart: 11, of which 3 were waited for; matrix products, arithmetic and copies ran while one was open for 9% of the time, Pallas kernels for 0%

profile of v1, /device:TPU:0, one launch (start us, length us, event | category | flops | bytes accessed | tf_op | source)
XLA Modules:
  0.0 76.2 jit_solution(8975359639936924700)
XLA Ops:
  0.7 5.0 %collective-permute-start = (bf16[1,256,256]{2,1,0:T(8,128)(2,1)}, bf16[1,256,256]{2,1,0:T(8,128)(2,1)S(1)}, u32[]{:S(2)}, u32[]{:S(2)}) collective-permute-start(bf16[1,256,256]{2,1,0:T(8,128)(2,1)} %bitcast.109), channel_id=1, source_target_pairs={{0,2},{2,4},{4,6},{6,8},{8,10},{10,12},{12,14},{1,3},{3,5},{5,7},{... | collective-permute-start | bytes 393224 | tf_op jit(solution)/shard_map/ppermute | solution.py:35
  5.7 1.3 %collective-permute-start.1 = (bf16[1,256,256]{2,1,0:T(8,128)(2,1)}, bf16[1,256,256]{2,1,0:T(8,128)(2,1)S(1)}, u32[]{:S(2)}, u32[]{:S(2)}) collective-permute-start(bf16[1,256,256]{2,1,0:T(8,128)(2,1)} %bitcast.110), channel_id=1, source_target_pairs={{2,0},{4,2},{6,4},{8,6},{10,8},{12,10},{14,12},{3,1},{5,3},{7,5},{... | collective-permute-start | bytes 393224 | tf_op jit(solution)/shard_map/ppermute | solution.py:37
  7.0 1.0 %fusion.56 = (bf16[1,255,256]{2,1,0:T(8,128)(2,1)S(1)}, bf16[1,255,256]{2,1,0:T(8,128)(2,1)S(1)}) fusion(bf16[1,256,256]{2,1,0:T(8,128)(2,1)} %bitcast.111), kind=kLoop, calls=%fused_computation.96 | loop fusion | bytes 522240 | tf_op jit(solution)/shard_map/jit(_roll_static)/slice | solution.py:61
  8.0 0.7 fusion.57
  8.7 0.8 %copy.56 = s32[1,256,2]{2,1,0:T(8,128)S(1)} copy(s32[1,256,2]{1,2,0:T(2,128)} %param.22) | data formatting | bytes 4096 | tf_op args[2]
  9.5 0.1 eq.89
  9.7 0.1 eq.85
  9.9 0.7 convert_element_type.74
  10.6 1.1 %reduce-window.6 = s32[8,4,128]{2,0,1:T(8,128)S(1)} reduce-window(s32[8,4,128]{2,0,1:T(8,128)S(1)} %fusion.41, s32[]{:T(128)} %constant.90.clone.1), window={size=1x1x128 pad=0_0x0_0x127_0}, to_apply=%region_4.5 | reduce-window | flops 520192 | bytes 32772 | tf_op jit(solution)/shard_map/reduce-window
  11.7 0.2 slice_reduce_fusion
  12.0 0.1 copy.68
  12.1 0.1 broadcast_in_dim_reshape.2
  12.3 0.1 mul.147
  12.4 0.1 mul.148
  12.5 0.1 copy.60
  12.7 0.1 mul.144
  12.8 0.1 fusion.40
  13.4 0.5 fusion.60
  13.9 22.0 %all-gather.1 = f32[8,1,256]{2,1,0:T(1,128)S(1)} all-gather(f32[1,1,256]{2,1,0:T(1,128)S(1)} %bitcast.127), channel_id=2, replica_groups=mesh['groups'=2,'space'=8,'section'=2] {'space'}, dimensions={0}, use_global_device_ids=true | all-gather | bytes 9216 | tf_op jit(solution)/shard_map/all_gather | solution.py:46
  35.9 0.1 fusion.61
  36.1 0.2 multiply_reduce_fusion
  36.3 0.6 fusion.18
  36.9 0.2 copy-done.3
  37.1 0.2 fusion.62
  37.3 0.1 mul.151
  37.4 1.6 %fusion.4 = bf16[1024,128]{1,0:T(8,128)(2,1)} fusion(s32[512]{0:T(512)S(1)} %multiply_add_fusion, f32[512,128]{1,0:T(8,128)S(1)} %bitcast.114, f32[512]{0:T(512)S(1)} %mul.149), kind=kOutput, calls=%fused_computation.8 | convolution fusion | flops 135004160 | bytes 528384 | tf_op jit(solution)/shard_map/dot_general | solution.py:79
  39.0 3.4 %all-to-all-start = ((bf16[8,128,128]{2,1,0:T(8,128)(2,1)}), bf16[8,128,128]{2,1,0:T(8,128)(2,1)S(1)}, u32[]{:S(2)}, u32[]{:S(2)}) async-start(bf16[8,128,128]{2,1,0:T(8,128)(2,1)} %bitcast.41), calls=%async_computation | async-start | bytes 524288 | tf_op jit(solution)/shard_map/all_to_all | solution.py:170
  42.4 0.3 select_reduce_fusion
  42.8 2.0 %collective-permute-start.2 = (s32[1,128]{1,0:T(1,128)S(1)}, s32[1,128]{1,0:T(1,128)S(1)}, u32[]{:S(2)}, u32[]{:S(2)}) collective-permute-start(s32[1,128]{1,0:T(1,128)S(1)} %get-tuple-element.52), channel_id=1, source_target_pairs={{0,2},{2,4},{4,6},{6,8},{8,10},{10,12},{12,14},{14,0},{1,3},{3,5},... | collective-permute-start | bytes 1544 | tf_op jit(solution)/shard_map/ppermute | solution.py:159
  44.7 1.5 %collective-permute-start.3 = (s32[1,128]{1,0:T(1,128)S(1)}, s32[1,128]{1,0:T(1,128)S(1)}, u32[]{:S(2)}, u32[]{:S(2)}) collective-permute-start(s32[1,128]{1,0:T(1,128)S(1)} %get-tuple-element.51), channel_id=1, source_target_pairs={{0,4},{2,6},{4,8},{6,10},{8,12},{10,14},{12,0},{14,2},{1,5},{3,7},... | collective-permute-start | bytes 1544 | tf_op jit(solution)/shard_map/ppermute | solution.py:159
  46.2 2.4 %collective-permute-start.4 = (s32[1,128]{1,0:T(1,128)S(1)}, s32[1,128]{1,0:T(1,128)S(1)}, u32[]{:S(2)}, u32[]{:S(2)}) collective-permute-start(s32[1,128]{1,0:T(1,128)S(1)} %get-tuple-element.50), channel_id=1, source_target_pairs={{0,6},{2,8},{4,10},{6,12},{8,14},{10,0},{12,2},{14,4},{1,7},{3,9},... | collective-permute-start | bytes 1544 | tf_op jit(solution)/shard_map/ppermute | solution.py:159
  48.6 1.4 %collective-permute-start.5 = (s32[1,128]{1,0:T(1,128)S(1)}, s32[1,128]{1,0:T(1,128)S(1)}, u32[]{:S(2)}, u32[]{:S(2)}) collective-permute-start(s32[1,128]{1,0:T(1,128)S(1)} %get-tuple-element.49), channel_id=1, source_target_pairs={{0,8},{2,10},{4,12},{6,14},{8,0},{10,2},{12,4},{14,6},{1,9},{3,11}... | collective-permute-start | bytes 1544 | tf_op jit(solution)/shard_map/ppermute | solution.py:159
  50.0 2.4 %collective-permute-start.6 = (s32[1,128]{1,0:T(1,128)S(1)}, s32[1,128]{1,0:T(1,128)S(1)}, u32[]{:S(2)}, u32[]{:S(2)}) collective-permute-start(s32[1,128]{1,0:T(1,128)S(1)} %get-tuple-element.48), channel_id=1, source_target_pairs={{0,10},{2,12},{4,14},{6,0},{8,2},{10,4},{12,6},{14,8},{1,11},{3,13... | collective-permute-start | bytes 1544 | tf_op jit(solution)/shard_map/ppermute | solution.py:159
  52.5 1.5 %collective-permute-start.7 = (s32[1,128]{1,0:T(1,128)S(1)}, s32[1,128]{1,0:T(1,128)S(1)}, u32[]{:S(2)}, u32[]{:S(2)}) collective-permute-start(s32[1,128]{1,0:T(1,128)S(1)} %get-tuple-element.47), channel_id=1, source_target_pairs={{0,12},{2,14},{4,0},{6,2},{8,4},{10,6},{12,8},{14,10},{1,13},{3,15... | collective-permute-start | bytes 1544 | tf_op jit(solution)/shard_map/ppermute | solution.py:159
  54.0 1.5 %collective-permute-start.8 = (s32[1,128]{1,0:T(1,128)S(1)}, s32[1,128]{1,0:T(1,128)S(1)}, u32[]{:S(2)}, u32[]{:S(2)}) collective-permute-start(s32[1,128]{1,0:T(1,128)S(1)} %get-tuple-element.46), channel_id=1, source_target_pairs={{0,14},{2,0},{4,2},{6,4},{8,6},{10,8},{12,10},{14,12},{1,15},{3,1}... | collective-permute-start | bytes 1544 | tf_op jit(solution)/shard_map/ppermute | solution.py:159
  55.4 0.6 collective-permute-done.7
  56.1 1.5 %collective-permute-done.8 = s32[1,128]{1,0:T(1,128)S(1)} collective-permute-done((s32[1,128]{1,0:T(1,128)S(1)}, s32[1,128]{1,0:T(1,128)S(1)}, u32[]{:S(2)}, u32[]{:S(2)}) %collective-permute-start.8) | collective-permute-done | bytes 544 | tf_op jit(solution)/shard_map/ppermute | solution.py:159
  57.6 0.6 gather_fusion
  58.1 0.8 %multiply_reduce_fusion.1 = (f32[256]{0:T(256)S(1)}, f32[256,192]{0,1:T(8,128)S(1)}) fusion(bf16[128,192]{0,1:T(8,128)(2,1)S(1)} %copy-done.12, bf16[1024,128]{1,0:T(8,128)(2,1)S(1)} %bitcast.115, s32[1024]{0:T(1024)S(1)} %bitcast.125, bf16[1,256,192]{1,2,0:T(8,128)(2,1)S(1)} %copy-done.11), kind=kOutput, calls=%fused_computation.38 | convolution fusion | flops 80183040 | bytes 611328 | tf_op jit(solution)/shard_map/dot_general | solution.py:185
  59.0 0.7 fusion.19
  59.7 0.1 copy-done.13
  59.8 1.2 %convolution_convert_fusion = bf16[1024,128]{1,0:T(8,128)(2,1)} fusion(bf16[256,192]{0,1:T(8,128)(2,1)S(1)} %fusion.19, bf16[192,128]{1,0:T(8,128)(2,1)S(1)} %copy-done.13, s32[1024]{0:T(1024)S(1)} %bitcast.126), kind=kOutput, calls=%fused_computation.9 | convolution fusion | flops 80117760 | bytes 413696 | tf_op jit(solution)/shard_map/dot_general | solution.py:198
  61.0 5.6 %all-to-all-start.1 = ((bf16[8,128,128]{2,1,0:T(8,128)(2,1)}), bf16[8,128,128]{2,1,0:T(8,128)(2,1)S(1)}, u32[]{:S(2)}, u32[]{:S(2)}) async-start(bf16[8,128,128]{2,1,0:T(8,128)(2,1)} %bitcast.43), calls=%async_computation.1 | async-start | bytes 524288 | tf_op jit(solution)/shard_map/all_to_all | solution.py:201
  66.6 0.1 reduce_sum.63
  66.8 0.1 copy.59
  66.8 8.0 %all-to-all-done.1 = bf16[8,128,128]{2,1,0:T(8,128)(2,1)S(1)} async-done(((bf16[8,128,128]{2,1,0:T(8,128)(2,1)}), bf16[8,128,128]{2,1,0:T(8,128)(2,1)S(1)}, u32[]{:S(2)}, u32[]{:S(2)}) %all-to-all-start.1) | async-done | bytes 262176 | tf_op jit(solution)/shard_map/all_to_all | solution.py:201
  74.8 0.5 fusion.15
  75.3 0.8 %fusion.20 = bf16[1,1,256,256]{3,2,1,0:T(8,128)(2,1)} fusion(bf16[128,256]{1,0:T(8,128)(2,1)S(1)} %copy-done.4, bf16[256,256]{1,0:T(8,128)(2,1)S(1)} %fusion.18, f32[256]{0:T(256)S(1)} %bitcast.121, bf16[256,128]{1,0:T(8,128)(2,1)S(1)} %fusion.15), kind=kOutput, calls=%fused_computation.23 | convolution fusion | flops 17039360 | bytes 394240 | tf_op jit(solution)/shard_map/dot_general | solution.py:211
  (70 shorter events, 0.5 us)
Async XLA Ops:
  0.6 12.7 %copy-start = (bf16[9,256,256]{2,1,0:T(8,128)(2,1)S(1)}, bf16[9,256,256]{2,1,0:T(8,128)(2,1)}, u32[]{:S(2)}) copy-start(bf16[9,256,256]{2,1,0:T(8,128)(2,1)} %param.26) | copy-start | bytes 3538948
  0.6 11.3 %copy-start.6 = (f32[1,256,2]{1,2,0:T(2,128)S(1)}, f32[1,256,2]{1,2,0:T(2,128)}, u32[]{:S(2)}) copy-start(f32[1,256,2]{1,2,0:T(2,128)} %param.24) | copy-start | bytes 6148
  0.7 11.9 %copy-start.5 = (s32[1,256,2]{1,2,0:T(2,128)S(1)}, s32[1,256,2]{1,2,0:T(2,128)}, u32[]{:S(2)}) copy-start(s32[1,256,2]{1,2,0:T(2,128)} %param.23) | copy-start | bytes 6148
  0.7 12.3 %collective-permute-start = (bf16[1,256,256]{2,1,0:T(8,128)(2,1)}, bf16[1,256,256]{2,1,0:T(8,128)(2,1)S(1)}, u32[]{:S(2)}, u32[]{:S(2)}) collective-permute-start(bf16[1,256,256]{2,1,0:T(8,128)(2,1)} %bitcast.109), channel_id=1, source_target_pairs={{0,2},{2,4},{4,6},{6,8},{8,10},{10,12},{12,14},{1,3},{3,5},{5,7},{... | collective-permute-start | bytes 393224 | tf_op jit(solution)/shard_map/ppermute | solution.py:35
  5.7 7.5 %collective-permute-start.1 = (bf16[1,256,256]{2,1,0:T(8,128)(2,1)}, bf16[1,256,256]{2,1,0:T(8,128)(2,1)S(1)}, u32[]{:S(2)}, u32[]{:S(2)}) collective-permute-start(bf16[1,256,256]{2,1,0:T(8,128)(2,1)} %bitcast.110), channel_id=1, source_target_pairs={{2,0},{4,2},{6,4},{8,6},{10,8},{12,10},{14,12},{3,1},{5,3},{7,5},{... | collective-permute-start | bytes 393224 | tf_op jit(solution)/shard_map/ppermute | solution.py:37
  12.1 1.0 %copy-start.1 = (bf16[1,1,256,256]{3,2,1,0:T(8,128)(2,1)S(1)}, bf16[1,1,256,256]{3,2,1,0:T(8,128)(2,1)}, u32[]{:S(2)}) copy-start(bf16[1,1,256,256]{3,2,1,0:T(8,128)(2,1)} %param.20) | copy-start | bytes 393220
  13.4 22.5 %copy-start.2 = (bf16[256,256]{1,0:T(8,128)(2,1)S(1)}, bf16[256,256]{1,0:T(8,128)(2,1)}, u32[]{:S(2)}) copy-start(bf16[256,256]{1,0:T(8,128)(2,1)} %param.27) | copy-start | bytes 393220
  13.4 22.9 %copy-start.7 = (bf16[1024,256]{1,0:T(8,128)(2,1)S(1)}, bf16[1024,256]{1,0:T(8,128)(2,1)}, u32[]{:S(2)}) copy-start(bf16[1024,256]{1,0:T(8,128)(2,1)} %param.30) | copy-start | bytes 1572868
  13.4 22.9 %copy-start.8 = (bf16[256,1024]{1,0:T(8,128)(2,1)S(1)}, bf16[256,1024]{1,0:T(8,128)(2,1)}, u32[]{:S(2)}) copy-start(bf16[256,1024]{1,0:T(8,128)(2,1)} %param.29) | copy-start | bytes 1572868
  13.4 22.9 %copy-start.14 = (f32[256]{0:T(256)S(1)}, f32[256]{0:T(256)}, u32[]{:S(2)}) copy-start(f32[256]{0:T(256)} %param.28) | copy-start | bytes 3076
  36.3 0.8 %copy-start.3 = (bf16[256,128]{1,0:T(8,128)(2,1)S(1)}, bf16[256,128]{1,0:T(8,128)(2,1)}, u32[]{:S(2)}) copy-start(bf16[256,128]{1,0:T(8,128)(2,1)} %param.31) | copy-start | bytes 196612
  37.1 21.0 %copy-start.11 = (bf16[1,256,192]{1,2,0:T(8,128)(2,1)S(1)}, bf16[1,256,192]{1,2,0:T(8,128)(2,1)}, u32[]{:S(2)}) copy-start(bf16[1,256,192]{1,2,0:T(8,128)(2,1)} %param.21) | copy-start | bytes 294916
  37.1 21.0 %copy-start.12 = (bf16[128,192]{0,1:T(8,128)(2,1)S(1)}, bf16[128,192]{0,1:T(8,128)(2,1)}, u32[]{:S(2)}) copy-start(bf16[128,192]{0,1:T(8,128)(2,1)} %param.32) | copy-start | bytes 147460
  37.4 21.6 %copy-start.9 = (bf16[768,192]{0,1:T(8,128)(2,1)S(1)}, bf16[768,192]{0,1:T(8,128)(2,1)}, u32[]{:S(2)}) copy-start(bf16[768,192]{0,1:T(8,128)(2,1)} %param.35) | copy-start | bytes 884740
  37.4 21.5 %copy-start.10 = (bf16[192,768]{1,0:T(8,128)(2,1)S(1)}, bf16[192,768]{1,0:T(8,128)(2,1)}, u32[]{:S(2)}) copy-start(bf16[192,768]{1,0:T(8,128)(2,1)} %param.34) | copy-start | bytes 884740
  37.4 21.5 %copy-start.15 = (f32[192]{0:T(256)S(1)}, f32[192]{0:T(256)}, u32[]{:S(2)}) copy-start(f32[192]{0:T(256)} %param.33) | copy-start | bytes 2308
  39.0 19.1 %all-to-all-start = ((bf16[8,128,128]{2,1,0:T(8,128)(2,1)}), bf16[8,128,128]{2,1,0:T(8,128)(2,1)S(1)}, u32[]{:S(2)}, u32[]{:S(2)}) async-start(bf16[8,128,128]{2,1,0:T(8,128)(2,1)} %bitcast.41), calls=%async_computation | async-start | bytes 524288 | tf_op jit(solution)/shard_map/all_to_all | solution.py:170
  42.8 9.7 %collective-permute-start.2 = (s32[1,128]{1,0:T(1,128)S(1)}, s32[1,128]{1,0:T(1,128)S(1)}, u32[]{:S(2)}, u32[]{:S(2)}) collective-permute-start(s32[1,128]{1,0:T(1,128)S(1)} %get-tuple-element.52), channel_id=1, source_target_pairs={{0,2},{2,4},{4,6},{6,8},{8,10},{10,12},{12,14},{14,0},{1,3},{3,5},... | collective-permute-start | bytes 1544 | tf_op jit(solution)/shard_map/ppermute | solution.py:159
  44.7 9.2 %collective-permute-start.3 = (s32[1,128]{1,0:T(1,128)S(1)}, s32[1,128]{1,0:T(1,128)S(1)}, u32[]{:S(2)}, u32[]{:S(2)}) collective-permute-start(s32[1,128]{1,0:T(1,128)S(1)} %get-tuple-element.51), channel_id=1, source_target_pairs={{0,4},{2,6},{4,8},{6,10},{8,12},{10,14},{12,0},{14,2},{1,5},{3,7},... | collective-permute-start | bytes 1544 | tf_op jit(solution)/shard_map/ppermute | solution.py:159
  46.2 9.2 %collective-permute-start.4 = (s32[1,128]{1,0:T(1,128)S(1)}, s32[1,128]{1,0:T(1,128)S(1)}, u32[]{:S(2)}, u32[]{:S(2)}) collective-permute-start(s32[1,128]{1,0:T(1,128)S(1)} %get-tuple-element.50), channel_id=1, source_target_pairs={{0,6},{2,8},{4,10},{6,12},{8,14},{10,0},{12,2},{14,4},{1,7},{3,9},... | collective-permute-start | bytes 1544 | tf_op jit(solution)/shard_map/ppermute | solution.py:159
  48.6 6.8 %collective-permute-start.5 = (s32[1,128]{1,0:T(1,128)S(1)}, s32[1,128]{1,0:T(1,128)S(1)}, u32[]{:S(2)}, u32[]{:S(2)}) collective-permute-start(s32[1,128]{1,0:T(1,128)S(1)} %get-tuple-element.49), channel_id=1, source_target_pairs={{0,8},{2,10},{4,12},{6,14},{8,0},{10,2},{12,4},{14,6},{1,9},{3,11}... | collective-permute-start | bytes 1544 | tf_op jit(solution)/shard_map/ppermute | solution.py:159
  50.0 5.4 %collective-permute-start.6 = (s32[1,128]{1,0:T(1,128)S(1)}, s32[1,128]{1,0:T(1,128)S(1)}, u32[]{:S(2)}, u32[]{:S(2)}) collective-permute-start(s32[1,128]{1,0:T(1,128)S(1)} %get-tuple-element.48), channel_id=1, source_target_pairs={{0,10},{2,12},{4,14},{6,0},{8,2},{10,4},{12,6},{14,8},{1,11},{3,13... | collective-permute-start | bytes 1544 | tf_op jit(solution)/shard_map/ppermute | solution.py:159
  52.5 3.6 %collective-permute-start.7 = (s32[1,128]{1,0:T(1,128)S(1)}, s32[1,128]{1,0:T(1,128)S(1)}, u32[]{:S(2)}, u32[]{:S(2)}) collective-permute-start(s32[1,128]{1,0:T(1,128)S(1)} %get-tuple-element.47), channel_id=1, source_target_pairs={{0,12},{2,14},{4,0},{6,2},{8,4},{10,6},{12,8},{14,10},{1,13},{3,15... | collective-permute-start | bytes 1544 | tf_op jit(solution)/shard_map/ppermute | solution.py:159
  54.0 3.6 %collective-permute-start.8 = (s32[1,128]{1,0:T(1,128)S(1)}, s32[1,128]{1,0:T(1,128)S(1)}, u32[]{:S(2)}, u32[]{:S(2)}) collective-permute-start(s32[1,128]{1,0:T(1,128)S(1)} %get-tuple-element.46), channel_id=1, source_target_pairs={{0,14},{2,0},{4,2},{6,4},{8,6},{10,8},{12,10},{14,12},{1,15},{3,1}... | collective-permute-start | bytes 1544 | tf_op jit(solution)/shard_map/ppermute | solution.py:159
  59.0 0.8 %copy-start.13 = (bf16[192,128]{1,0:T(8,128)(2,1)S(1)}, bf16[192,128]{1,0:T(8,128)(2,1)}, u32[]{:S(2)}) copy-start(bf16[192,128]{1,0:T(8,128)(2,1)} %param.36) | copy-start | bytes 147460
  59.8 15.6 %copy-start.16 = (bf16[256,192]{0,1:T(8,128)(2,1)}, bf16[256,192]{0,1:T(8,128)(2,1)S(1)}, u32[]{:S(2)}) copy-start(bf16[256,192]{0,1:T(8,128)(2,1)S(1)} %fusion.19) | copy-start | bytes 294916
  61.0 14.3 %copy-start.4 = (bf16[128,256]{1,0:T(8,128)(2,1)S(1)}, bf16[128,256]{1,0:T(8,128)(2,1)}, u32[]{:S(2)}) copy-start(bf16[128,256]{1,0:T(8,128)(2,1)} %param.37) | copy-start | bytes 196612
  61.0 13.8 %all-to-all-start.1 = ((bf16[8,128,128]{2,1,0:T(8,128)(2,1)}), bf16[8,128,128]{2,1,0:T(8,128)(2,1)S(1)}, u32[]{:S(2)}, u32[]{:S(2)}) async-start(bf16[8,128,128]{2,1,0:T(8,128)(2,1)} %bitcast.43), calls=%async_computation.1 | async-start | bytes 524288 | tf_op jit(solution)/shard_map/all_to_all | solution.py:201
